TPU v7x, 256 devices: a whole 4x4x8 slice. The times are simulated.
256 devices in a mesh: row: 16 (over x, z_lo, core), col: 16 (over z_hi, y).
Axes of the slice: x: 4, y: 4, z: 8 (z_hi: 4, z_lo: 2; z = z_hi * 2 + z_lo), core: 2. Of those that a mesh axis runs over, the one named last changes fastest.
Arguments:
- iterate: bfloat16 [4096, 8192], P('row', 'col'), may hold values from -0.5 to 0.5, as said below
Outputs:
- update: float32 [4096, 8192], P('row', 'col')
Inputs may be any that keep to these rules, and one draw needn't show every extreme that they name: One iterate of the orthogonalization.
All inputs are finite; a program needn't handle non-finite values.
Results may differ from a plain program's by a relative error of at most 0.0041.
Values may be sent and summed in bfloat16 or wider, within the bound.
No kernel may reach another device: no remote copies, remote signals or barrier semaphores. Data moves between devices by JAX's collectives and lax.ppermute only.
A program may use at most 64 MiB of HBM per device.

v0:
```python
import math
import jax
import jax.numpy as jnp
from jax import lax
from jax.sharding import Mesh
from jax.sharding import PartitionSpec as P

COLS = 8192
coef_a = 3.4445
coef_b = -4.775
coef_c = 2.0315
ROW = ("x", "zl", "core")
COL = ("zh", "y")
BF, F32 = (jnp.bfloat16, jnp.float32)


def swap(array, axis):
    return lax.ppermute(array, axis, [(0, 1), (1, 0)])


def send(array, axis, k):
    return lax.ppermute(array, axis, [(i, (i + k) % 4) for i in range(4)]) if k else array


def fetch(array, axis, k):
    return send(array, axis, (4 - k) % 4)


def add(got):
    got = [g.astype(F32) for g in got]
    return (got[0] + got[1] + (got[2] + got[3])).astype(BF)


def trade(array, axis, k):
    return lax.ppermute(array, axis, [(i, i ^ k) for i in range(4)])


def scatter_pairs(pieces, axis):
    return [pieces[0]] + [trade(pieces[k], axis, k) for k in (1, 3, 2)]


def chunks(array):
    return jnp.split(array, 4, axis=0)


def window(parts, first, count):
    rows = parts[0].shape[0]
    ring = jnp.concatenate([*parts, *parts[: count - 1]], axis=0)
    return lax.dynamic_slice_in_dim(ring, first * rows, count * rows, 0)


def matmul(a, b, dims):
    return lax.dot_general(a, b, (dims, ((), ())), preferred_element_type=F32)


def pair_of(block):
    far = fetch(block, "x", 2)
    return (jnp.concatenate([block, swap(block, "zl")], axis=0), far)


def late_blocks(pair, far):
    return [trade(pair, "x", 1), trade(pair, "x", 3), swap(far, "zl")]


def core_sum(products):
    mine = jnp.concatenate([m for m, _ in products], axis=0)
    other = jnp.concatenate([o for _, o in products], axis=0)
    return mine + swap(other, "core")


def per_device(iterate):
    y, zh = (lax.axis_index("y"), lax.axis_index("zh"))
    back = lax.rem(4 - y, 4)
    other = swap(iterate, "core")
    pair, far = pair_of(iterate)
    own = [jnp.concatenate(rows, axis=0) for rows in zip(chunks(iterate), chunks(other))]
    own = jnp.stack(own).reshape(4, 4, 32, 512)
    own = [lax.dynamic_slice_in_dim(own, zh ^ k, 1, 1) for k in range(4)]
    own = jnp.concatenate(own, axis=1).reshape(512, 512)
    turned = [lax.dynamic_slice_in_dim(own, (y ^ k) * 128, 128) for k in range(4)]
    turned = jnp.concatenate(turned, axis=0)
    pair, own, turned = lax.optimization_barrier((pair, own, turned))
    early = lax.optimization_barrier(jnp.concatenate([pair, far], axis=0))
    pieces = matmul(own, early, ((1,), (1,))).astype(BF)
    late = late_blocks(pair, far)
    first = add(lax.all_to_all(pieces.reshape(4, 128, 768), "y", 0, 0))
    panel = lax.optimization_barrier(jnp.concatenate(late, axis=0))
    pieces = [matmul(rows, panel, ((1,), (1,))).astype(BF) for rows in chunks(turned)]
    pieces[0] = lax.optimization_barrier(pieces[0])
    second = add(scatter_pairs(pieces, "y"))
    part = jnp.concatenate([first, second], axis=1)
    panel = jnp.concatenate([early, panel], axis=0)
    part = add(scatter_pairs(chunks(part), "zh"))
    near = lax.all_gather(part, "zh", axis=0, tiled=True)
    after, before = (fetch(near, "y", 1), fetch(near, "y", 3))
    sent = lax.optimization_barrier((after[:64], before[64:]))
    far = lax.optimization_barrier((fetch(sent[0], "y", 1), fetch(sent[1], "y", 3)))

    def product(rows):
        return matmul(rows, panel, ((1,), (0,)))

    first = core_sum([(m[:64], m[64:]) for m in map(product, (near, after, before))])
    second = core_sum([(product(far[0]), product(far[1]))])
    inner = window([first[:64], first[64:128], second, first[128:]], back, 4)
    pair, last = pair_of(inner.astype(BF))
    pair, *late = lax.optimization_barrier([pair, last, *late_blocks(pair, last)])
    panels = (jnp.concatenate([pair, late[0]], axis=0), jnp.concatenate(late[1:], axis=0))
    gram = [(near[:64], near[64:]), (after[:64], after[64:]), far, (before[:64], before[64:])]
    mixed = []
    for rows in zip(*gram):
        rows = window(rows, back, 4)
        halves = (rows[:, :768], rows[:, 768:])
        mixed.append(sum((matmul(h, panel, ((1,), (0,))) for h, panel in zip(halves, panels))))
    mixed = mixed[0] + swap(mixed[1], "core")
    mine = iterate.astype(F32)
    return math.sqrt(COLS) * (coef_a * mine + (coef_b * inner + coef_c * mixed))


def solution(mesh):
    fine = Mesh(mesh.devices.reshape(4, 2, 2, 4, 4), (*ROW, *COL))
    placed = P(ROW, COL)
    return jax.shard_map(
        per_device, mesh=fine, in_specs=(placed,), out_specs=placed, check_vma=False
    )
```

profile of v0, /device:TPU:1, one launch (start us, length us, event | category | flops | bytes accessed | tf_op | source)
XLA Modules:
  0.0 139.4 jit_solution(9716099758347293773)
XLA Ops:
  0.0 3.2 %collective-permute-start.1 = (bf16[256,512]{1,0:T(8,128)(2,1)}, bf16[256,512]{1,0:T(8,128)(2,1)S(1)}, u32[]{:S(2)}, u32[]{:S(2)}) collective-permute-start(bf16[256,512]{1,0:T(8,128)(2,1)} %param.1), channel_id=1, source_target_pairs={{0,16},{16,0},{1,17},{17,1},{2,18},{18,2},{3,19},{19,3},{4,20},{20... | collective-permute-start | bytes 786440 | tf_op jit(solution)/shard_map/ppermute | solution.py:18
  3.2 2.6 %collective-permute-start.2 = (bf16[256,512]{1,0:T(8,128)(2,1)}, bf16[256,512]{1,0:T(8,128)(2,1)}, u32[]{:S(2)}, u32[]{:S(2)}) collective-permute-start(bf16[256,512]{1,0:T(8,128)(2,1)} %param.1), channel_id=1, source_target_pairs={{0,128},{64,192},{128,0},{192,64},{1,129},{65,193},{129,1},{193,65... | collective-permute-start | bytes 786440 | tf_op jit(solution)/shard_map/ppermute | solution.py:22
  7.3 4.2 %collective-permute-done = bf16[256,512]{1,0:T(8,128)(2,1)S(1)} collective-permute-done((bf16[256,512]{1,0:T(8,128)(2,1)}, bf16[256,512]{1,0:T(8,128)(2,1)S(1)}, u32[]{:S(2)}, u32[]{:S(2)}) %collective-permute-start) | collective-permute-done | bytes 262176 | tf_op jit(solution)/shard_map/ppermute | solution.py:18
  11.6 1.6 %collective-permute-start.4 = (bf16[512,512]{1,0:T(8,128)(2,1)S(1)}, bf16[512,512]{1,0:T(8,128)(2,1)}, u32[]{:S(2)}, u32[]{:S(2)}) collective-permute-start(bf16[512,512]{1,0:T(8,128)(2,1)S(1)} %pad_maximum_fusion.3), channel_id=1, source_target_pairs={{0,192},{64,128},{128,64},{192,0},{1,193},{65,129},{129,65},{193,1... | collective-permute-start | bytes 1572872 | tf_op jit(solution)/shard_map/ppermute | solution.py:35
  14.2 1.5 %collective-permute-start.5 = (bf16[256,512]{1,0:T(8,128)(2,1)}, bf16[256,512]{1,0:T(8,128)(2,1)}, u32[]{:S(2)}, u32[]{:S(2)}) collective-permute-start(bf16[256,512]{1,0:T(8,128)(2,1)} %collective-permute-done.2), channel_id=1, source_target_pairs={{0,32},{32,0},{1,33},{33,1},{2,34},{34,2},{3,35},{35,3},{4,36},{36... | collective-permute-start | bytes 786440 | tf_op jit(solution)/shard_map/ppermute | solution.py:18
  15.7 1.5 %convolution_convert_fusion.4 = bf16[512,768]{1,0:T(8,128)(2,1)} fusion(bf16[512,512]{1,0:T(8,128)(2,1)S(1)} %bitcast.24, bf16[768,512]{1,0:T(8,128)(2,1)S(1)} %pad_maximum_fusion.2), kind=kOutput, calls=%fused_computation.5 | convolution fusion | flops 403046400 | bytes 2097152 | tf_op jit(solution)/shard_map/dot_general | solution.py:53
  17.2 4.2 %all-to-all-start = ((bf16[4,128,768]{2,1,0:T(8,128)(2,1)}), bf16[4,128,768]{2,1,0:T(8,128)(2,1)S(1)}, u32[]{:S(2)}, u32[]{:S(2)}) async-start(bf16[4,128,768]{2,1,0:T(8,128)(2,1)} %bitcast.25), calls=%async_computation | async-start | bytes 1572864 | tf_op jit(solution)/shard_map/all_to_all | solution.py:86
  21.3 3.2 %collective-permute-done.3 = bf16[512,512]{1,0:T(8,128)(2,1)S(1)} collective-permute-done((bf16[512,512]{1,0:T(8,128)(2,1)S(1)}, bf16[512,512]{1,0:T(8,128)(2,1)S(1)}, u32[]{:S(2)}, u32[]{:S(2)}) %collective-permute-start.3) | collective-permute-done | bytes 524320 | tf_op jit(solution)/shard_map/ppermute | solution.py:35
  24.5 1.3 collective-permute-done.4
  27.0 1.3 convolution_convert_fusion.2
  29.7 1.9 %collective-permute-start.7 = (bf16[128,1280]{1,0:T(8,128)(2,1)S(1)}, bf16[128,1280]{1,0:T(8,128)(2,1)}, u32[]{:S(2)}, u32[]{:S(2)}) collective-permute-start(bf16[128,1280]{1,0:T(8,128)(2,1)S(1)} %convolution_convert_fusion.1), channel_id=1, source_target_pairs={{0,3},{1,2},{2,1},{3,0},{4,7},{5,6},{6,5},{7,4},{8,11},{9,10},{10,... | collective-permute-start | bytes 983048 | tf_op jit(solution)/shard_map/ppermute | solution.py:35
  31.6 1.3 convolution_convert_fusion
  34.3 4.2 %collective-permute-done.6 = bf16[128,1280]{1,0:T(8,128)(2,1)} collective-permute-done((bf16[128,1280]{1,0:T(8,128)(2,1)}, bf16[128,1280]{1,0:T(8,128)(2,1)}, u32[]{:S(2)}, u32[]{:S(2)}) %collective-permute-start.6) | collective-permute-done | bytes 327712 | tf_op jit(solution)/shard_map/ppermute | solution.py:35
  39.3 7.1 %collective-permute-done.8 = bf16[128,1280]{1,0:T(8,128)(2,1)} collective-permute-done((bf16[128,1280]{1,0:T(8,128)(2,1)}, bf16[128,1280]{1,0:T(8,128)(2,1)}, u32[]{:S(2)}, u32[]{:S(2)}) %collective-permute-start.8) | collective-permute-done | bytes 327712 | tf_op jit(solution)/shard_map/ppermute | solution.py:35
  46.4 1.3 add_convert_fusion
  47.8 4.8 %collective-permute-start.10 = (bf16[32,2048]{1,0:T(8,128)(2,1)S(1)}, bf16[32,2048]{1,0:T(8,128)(2,1)S(1)}, u32[]{:S(2)}, u32[]{:S(2)}) collective-permute-start(bf16[32,2048]{1,0:T(8,128)(2,1)S(1)} %get-tuple-element.37), channel_id=1, source_target_pairs={{0,12},{4,8},{8,4},{12,0},{1,13},{5,9},{9,5},{13,1},{2,14},{6,10},... | collective-permute-start | bytes 393224 | tf_op jit(solution)/shard_map/ppermute | solution.py:35
  52.6 1.6 %collective-permute-start.11 = (bf16[32,2048]{1,0:T(8,128)(2,1)S(1)}, bf16[32,2048]{1,0:T(8,128)(2,1)S(1)}, u32[]{:S(2)}, u32[]{:S(2)}) collective-permute-start(bf16[32,2048]{1,0:T(8,128)(2,1)S(1)} %get-tuple-element.36), channel_id=1, source_target_pairs={{0,8},{4,12},{8,0},{12,4},{1,9},{5,13},{9,1},{13,5},{2,10},{6,14},... | collective-permute-start | bytes 393224 | tf_op jit(solution)/shard_map/ppermute | solution.py:35
  54.8 7.4 %collective-permute-done.10 = bf16[32,2048]{1,0:T(8,128)(2,1)S(1)} collective-permute-done((bf16[32,2048]{1,0:T(8,128)(2,1)S(1)}, bf16[32,2048]{1,0:T(8,128)(2,1)S(1)}, u32[]{:S(2)}, u32[]{:S(2)}) %collective-permute-start.10) | collective-permute-done | bytes 131104 | tf_op jit(solution)/shard_map/ppermute | solution.py:35
  64.2 15.8 %all_gather.3 = bf16[128,2048]{1,0:T(8,128)(2,1)S(1)} all-gather(bf16[32,2048]{1,0:T(8,128)(2,1)S(1)} %add_convert_fusion.2), channel_id=1, replica_groups=mesh['x'=4,'zl'=2,'core'=2,'zh'=4,'y'=4] {'zh'}, dimensions={0}, use_global_device_ids=true | all-gather | bytes 655360 | tf_op jit(solution)/shard_map/all_gather | solution.py:94
  80.0 1.5 %collective-permute-start.12 = (bf16[128,2048]{1,0:T(8,128)(2,1)S(1)}, bf16[128,2048]{1,0:T(8,128)(2,1)S(1)}, u32[]{:S(2)}, u32[]{:S(2)}) collective-permute-start(bf16[128,2048]{1,0:T(8,128)(2,1)S(1)} %all_gather.3), channel_id=1, source_target_pairs={{0,3},{1,0},{2,1},{3,2},{4,7},{5,4},{6,5},{7,6},{8,11},{9,8},{10,9... | collective-permute-start | bytes 1572872 | tf_op jit(solution)/shard_map/ppermute | solution.py:22
  81.5 3.4 %collective-permute-start.13 = (bf16[128,2048]{1,0:T(8,128)(2,1)S(1)}, bf16[128,2048]{1,0:T(8,128)(2,1)S(1)}, u32[]{:S(2)}, u32[]{:S(2)}) collective-permute-start(bf16[128,2048]{1,0:T(8,128)(2,1)S(1)} %all_gather.3), channel_id=1, source_target_pairs={{0,1},{1,2},{2,3},{3,0},{4,5},{5,6},{6,7},{7,4},{8,9},{9,10},{10,1... | collective-permute-start | bytes 1572872 | tf_op jit(solution)/shard_map/ppermute | solution.py:22
  85.5 7.4 %collective-permute-done.13 = bf16[128,2048]{1,0:T(8,128)(2,1)S(1)} collective-permute-done((bf16[128,2048]{1,0:T(8,128)(2,1)S(1)}, bf16[128,2048]{1,0:T(8,128)(2,1)S(1)}, u32[]{:S(2)}, u32[]{:S(2)}) %collective-permute-start.13) | collective-permute-done | bytes 524320 | tf_op jit(solution)/shard_map/ppermute | solution.py:22
  94.0 1.9 %collective-permute-start.15 = (bf16[64,2048]{1,0:T(8,128)(2,1)S(1)}, bf16[64,2048]{1,0:T(8,128)(2,1)S(1)}, u32[]{:S(2)}, u32[]{:S(2)}) collective-permute-start(bf16[64,2048]{1,0:T(8,128)(2,1)S(1)} %get-tuple-element.20), channel_id=1, source_target_pairs={{0,3},{1,0},{2,1},{3,2},{4,7},{5,4},{6,5},{7,6},{8,11},{9,8},{10,9... | collective-permute-start | bytes 786440 | tf_op jit(solution)/shard_map/ppermute | solution.py:22
  96.9 5.3 %collective-permute-start.14 = (f32[192,512]{1,0:T(8,128)S(1)}, f32[192,512]{1,0:T(8,128)S(1)}, u32[]{:S(2)}, u32[]{:S(2)}) collective-permute-start(f32[192,512]{1,0:T(8,128)S(1)} %pad_maximum_fusion.8), channel_id=1, source_target_pairs={{0,16},{16,0},{1,17},{17,1},{2,18},{18,2},{3,19},{19,3},{4,20},{20... | collective-permute-start | bytes 1179656 | tf_op jit(solution)/shard_map/ppermute | solution.py:18
  102.9 5.7 %collective-permute-start.17 = (f32[64,512]{1,0:T(8,128)S(1)}, f32[64,512]{1,0:T(8,128)S(1)}, u32[]{:S(2)}, u32[]{:S(2)}) collective-permute-start(f32[64,512]{1,0:T(8,128)S(1)} %fusion.20), channel_id=1, source_target_pairs={{0,16},{16,0},{1,17},{17,1},{2,18},{18,2},{3,19},{19,3},{4,20},{20... | collective-permute-start | bytes 393224 | tf_op jit(solution)/shard_map/ppermute | solution.py:18
  110.6 4.1 %collective-permute-start.19 = (bf16[256,512]{1,0:T(8,128)(2,1)S(1)}, bf16[256,512]{1,0:T(8,128)(2,1)S(1)}, u32[]{:S(2)}, u32[]{:S(2)}) collective-permute-start(bf16[256,512]{1,0:T(8,128)(2,1)S(1)} %dynamic-slice_convert_fusion), channel_id=1, source_target_pairs={{0,128},{64,192},{128,0},{192,64},{1,129},{65,193},{129,1},{193,65... | collective-permute-start | bytes 786440 | tf_op jit(solution)/shard_map/ppermute | solution.py:22
  114.7 3.1 %collective-permute-done.18 = bf16[256,512]{1,0:T(8,128)(2,1)S(1)} collective-permute-done((bf16[256,512]{1,0:T(8,128)(2,1)S(1)}, bf16[256,512]{1,0:T(8,128)(2,1)S(1)}, u32[]{:S(2)}, u32[]{:S(2)}) %collective-permute-start.18) | collective-permute-done | bytes 262176 | tf_op jit(solution)/shard_map/ppermute | solution.py:18
  119.0 3.5 %collective-permute-start.21 = (bf16[512,512]{1,0:T(8,128)(2,1)S(1)}, bf16[512,512]{1,0:T(8,128)(2,1)S(1)}, u32[]{:S(2)}, u32[]{:S(2)}) collective-permute-start(bf16[512,512]{1,0:T(8,128)(2,1)S(1)} %pad_maximum_fusion.7), channel_id=1, source_target_pairs={{0,192},{64,128},{128,64},{192,0},{1,193},{65,129},{129,65},{193,1... | collective-permute-start | bytes 1572872 | tf_op jit(solution)/shard_map/ppermute | solution.py:35
  122.9 5.7 %collective-permute-done.22 = bf16[256,512]{1,0:T(8,128)(2,1)S(1)} collective-permute-done((bf16[256,512]{1,0:T(8,128)(2,1)S(1)}, bf16[256,512]{1,0:T(8,128)(2,1)S(1)}, u32[]{:S(2)}, u32[]{:S(2)}) %collective-permute-start.22) | collective-permute-done | bytes 262176 | tf_op jit(solution)/shard_map/ppermute | solution.py:18
  128.6 2.7 %collective-permute-done.20 = bf16[512,512]{1,0:T(8,128)(2,1)S(1)} collective-permute-done((bf16[512,512]{1,0:T(8,128)(2,1)S(1)}, bf16[512,512]{1,0:T(8,128)(2,1)S(1)}, u32[]{:S(2)}, u32[]{:S(2)}) %collective-permute-start.20) | collective-permute-done | bytes 524320 | tf_op jit(solution)/shard_map/ppermute | solution.py:35
  131.3 2.0 %collective-permute-done.21 = bf16[512,512]{1,0:T(8,128)(2,1)S(1)} collective-permute-done((bf16[512,512]{1,0:T(8,128)(2,1)S(1)}, bf16[512,512]{1,0:T(8,128)(2,1)S(1)}, u32[]{:S(2)}, u32[]{:S(2)}) %collective-permute-start.21) | collective-permute-done | bytes 524320 | tf_op jit(solution)/shard_map/ppermute | solution.py:35
  134.4 2.2 %collective-permute-start.23 = (f32[256,512]{1,0:T(8,128)S(1)}, f32[256,512]{1,0:T(8,128)S(1)}, u32[]{:S(2)}, u32[]{:S(2)}) collective-permute-start(f32[256,512]{1,0:T(8,128)S(1)} %convolution_add_fusion), channel_id=1, source_target_pairs={{0,16},{16,0},{1,17},{17,1},{2,18},{18,2},{3,19},{19,3},{4,20},{20... | collective-permute-start | bytes 1572872 | tf_op jit(solution)/shard_map/ppermute | solution.py:18
  (84 shorter events, 20.4 us)
Async XLA Ops:
  0.0 6.8 %collective-permute-start.1 = (bf16[256,512]{1,0:T(8,128)(2,1)}, bf16[256,512]{1,0:T(8,128)(2,1)S(1)}, u32[]{:S(2)}, u32[]{:S(2)}) collective-permute-start(bf16[256,512]{1,0:T(8,128)(2,1)} %param.1), channel_id=1, source_target_pairs={{0,16},{16,0},{1,17},{17,1},{2,18},{18,2},{3,19},{19,3},{4,20},{20... | collective-permute-start | bytes 786440 | tf_op jit(solution)/shard_map/ppermute | solution.py:18
  3.2 8.3 %collective-permute-start = (bf16[256,512]{1,0:T(8,128)(2,1)}, bf16[256,512]{1,0:T(8,128)(2,1)S(1)}, u32[]{:S(2)}, u32[]{:S(2)}) collective-permute-start(bf16[256,512]{1,0:T(8,128)(2,1)} %param.1), channel_id=1, source_target_pairs={{0,32},{32,0},{1,33},{33,1},{2,34},{34,2},{3,35},{35,3},{4,36},{36... | collective-permute-start | bytes 786440 | tf_op jit(solution)/shard_map/ppermute | solution.py:18
  3.2 9.9 %collective-permute-start.2 = (bf16[256,512]{1,0:T(8,128)(2,1)}, bf16[256,512]{1,0:T(8,128)(2,1)}, u32[]{:S(2)}, u32[]{:S(2)}) collective-permute-start(bf16[256,512]{1,0:T(8,128)(2,1)} %param.1), channel_id=1, source_target_pairs={{0,128},{64,192},{128,0},{192,64},{1,129},{65,193},{129,1},{193,65... | collective-permute-start | bytes 786440 | tf_op jit(solution)/shard_map/ppermute | solution.py:22
  7.1 4.4 %copy-start = (bf16[256,512]{1,0:T(8,128)(2,1)S(1)}, bf16[256,512]{1,0:T(8,128)(2,1)}, u32[]{:S(2)}) copy-start(bf16[256,512]{1,0:T(8,128)(2,1)} %param.1) | copy-start | bytes 786436
  11.5 13.0 %collective-permute-start.3 = (bf16[512,512]{1,0:T(8,128)(2,1)S(1)}, bf16[512,512]{1,0:T(8,128)(2,1)S(1)}, u32[]{:S(2)}, u32[]{:S(2)}) collective-permute-start(bf16[512,512]{1,0:T(8,128)(2,1)S(1)} %pad_maximum_fusion.3), channel_id=1, source_target_pairs={{0,64},{64,0},{128,192},{192,128},{1,65},{65,1},{129,193},{193,129... | collective-permute-start | bytes 1572872 | tf_op jit(solution)/shard_map/ppermute | solution.py:35
  11.6 14.2 %collective-permute-start.4 = (bf16[512,512]{1,0:T(8,128)(2,1)S(1)}, bf16[512,512]{1,0:T(8,128)(2,1)}, u32[]{:S(2)}, u32[]{:S(2)}) collective-permute-start(bf16[512,512]{1,0:T(8,128)(2,1)S(1)} %pad_maximum_fusion.3), channel_id=1, source_target_pairs={{0,192},{64,128},{128,64},{192,0},{1,193},{65,129},{129,65},{193,1... | collective-permute-start | bytes 1572872 | tf_op jit(solution)/shard_map/ppermute | solution.py:35
  14.2 3.0 %copy-start.1 = (bf16[768,512]{1,0:T(8,128)(2,1)}, bf16[768,512]{1,0:T(8,128)(2,1)S(1)}, u32[]{:S(2)}) copy-start(bf16[768,512]{1,0:T(8,128)(2,1)S(1)} %pad_maximum_fusion.2) | copy-start | bytes 2359300
  14.2 7.1 %collective-permute-start.5 = (bf16[256,512]{1,0:T(8,128)(2,1)}, bf16[256,512]{1,0:T(8,128)(2,1)}, u32[]{:S(2)}, u32[]{:S(2)}) collective-permute-start(bf16[256,512]{1,0:T(8,128)(2,1)} %collective-permute-done.2), channel_id=1, source_target_pairs={{0,32},{32,0},{1,33},{33,1},{2,34},{34,2},{3,35},{35,3},{4,36},{36... | collective-permute-start | bytes 786440 | tf_op jit(solution)/shard_map/ppermute | solution.py:18
  17.2 17.0 %all-to-all-start = ((bf16[4,128,768]{2,1,0:T(8,128)(2,1)}), bf16[4,128,768]{2,1,0:T(8,128)(2,1)S(1)}, u32[]{:S(2)}, u32[]{:S(2)}) async-start(bf16[4,128,768]{2,1,0:T(8,128)(2,1)} %bitcast.25), calls=%async_computation | async-start | bytes 1572864 | tf_op jit(solution)/shard_map/all_to_all | solution.py:86
  28.9 9.6 %collective-permute-start.6 = (bf16[128,1280]{1,0:T(8,128)(2,1)}, bf16[128,1280]{1,0:T(8,128)(2,1)}, u32[]{:S(2)}, u32[]{:S(2)}) collective-permute-start(bf16[128,1280]{1,0:T(8,128)(2,1)} %convolution_convert_fusion.2), channel_id=1, source_target_pairs={{0,1},{1,0},{2,3},{3,2},{4,5},{5,4},{6,7},{7,6},{8,9},{9,8},{10,11... | collective-permute-start | bytes 983048 | tf_op jit(solution)/shard_map/ppermute | solution.py:35
  29.7 9.6 %collective-permute-start.7 = (bf16[128,1280]{1,0:T(8,128)(2,1)S(1)}, bf16[128,1280]{1,0:T(8,128)(2,1)}, u32[]{:S(2)}, u32[]{:S(2)}) collective-permute-start(bf16[128,1280]{1,0:T(8,128)(2,1)S(1)} %convolution_convert_fusion.1), channel_id=1, source_target_pairs={{0,3},{1,2},{2,1},{3,0},{4,7},{5,6},{6,5},{7,4},{8,11},{9,10},{10,... | collective-permute-start | bytes 983048 | tf_op jit(solution)/shard_map/ppermute | solution.py:35
  32.9 13.6 %collective-permute-start.8 = (bf16[128,1280]{1,0:T(8,128)(2,1)}, bf16[128,1280]{1,0:T(8,128)(2,1)}, u32[]{:S(2)}, u32[]{:S(2)}) collective-permute-start(bf16[128,1280]{1,0:T(8,128)(2,1)} %convolution_convert_fusion), channel_id=1, source_target_pairs={{0,2},{1,3},{2,0},{3,1},{4,6},{5,7},{6,4},{7,5},{8,10},{9,11},{10,... | collective-permute-start | bytes 983048 | tf_op jit(solution)/shard_map/ppermute | solution.py:35
  34.3 50.7 %copy-start.2 = (bf16[768,512]{1,0:T(8,128)(2,1)S(1)}, bf16[768,512]{1,0:T(8,128)(2,1)}, u32[]{:S(2)}) copy-start(bf16[768,512]{1,0:T(8,128)(2,1)} %copy-done.1) | copy-start | bytes 2359300
  47.8 14.3 %collective-permute-start.10 = (bf16[32,2048]{1,0:T(8,128)(2,1)S(1)}, bf16[32,2048]{1,0:T(8,128)(2,1)S(1)}, u32[]{:S(2)}, u32[]{:S(2)}) collective-permute-start(bf16[32,2048]{1,0:T(8,128)(2,1)S(1)} %get-tuple-element.37), channel_id=1, source_target_pairs={{0,12},{4,8},{8,4},{12,0},{1,13},{5,9},{9,5},{13,1},{2,14},{6,10},... | collective-permute-start | bytes 393224 | tf_op jit(solution)/shard_map/ppermute | solution.py:35
  52.6 9.8 %collective-permute-start.11 = (bf16[32,2048]{1,0:T(8,128)(2,1)S(1)}, bf16[32,2048]{1,0:T(8,128)(2,1)S(1)}, u32[]{:S(2)}, u32[]{:S(2)}) collective-permute-start(bf16[32,2048]{1,0:T(8,128)(2,1)S(1)} %get-tuple-element.36), channel_id=1, source_target_pairs={{0,8},{4,12},{8,0},{12,4},{1,9},{5,13},{9,1},{13,5},{2,10},{6,14},... | collective-permute-start | bytes 393224 | tf_op jit(solution)/shard_map/ppermute | solution.py:35
  54.2 9.1 %collective-permute-start.9 = (bf16[32,2048]{1,0:T(8,128)(2,1)S(1)}, bf16[32,2048]{1,0:T(8,128)(2,1)}, u32[]{:S(2)}, u32[]{:S(2)}) collective-permute-start(bf16[32,2048]{1,0:T(8,128)(2,1)S(1)} %get-tuple-element.35), channel_id=1, source_target_pairs={{0,4},{4,0},{8,12},{12,8},{1,5},{5,1},{9,13},{13,9},{2,6},{6,2},{1... | collective-permute-start | bytes 393224 | tf_op jit(solution)/shard_map/ppermute | solution.py:35
  80.0 13.9 %collective-permute-start.12 = (bf16[128,2048]{1,0:T(8,128)(2,1)S(1)}, bf16[128,2048]{1,0:T(8,128)(2,1)S(1)}, u32[]{:S(2)}, u32[]{:S(2)}) collective-permute-start(bf16[128,2048]{1,0:T(8,128)(2,1)S(1)} %all_gather.3), channel_id=1, source_target_pairs={{0,3},{1,0},{2,1},{3,2},{4,7},{5,4},{6,5},{7,6},{8,11},{9,8},{10,9... | collective-permute-start | bytes 1572872 | tf_op jit(solution)/shard_map/ppermute | solution.py:22
  81.5 11.4 %collective-permute-start.13 = (bf16[128,2048]{1,0:T(8,128)(2,1)S(1)}, bf16[128,2048]{1,0:T(8,128)(2,1)S(1)}, u32[]{:S(2)}, u32[]{:S(2)}) collective-permute-start(bf16[128,2048]{1,0:T(8,128)(2,1)S(1)} %all_gather.3), channel_id=1, source_target_pairs={{0,1},{1,2},{2,3},{3,0},{4,5},{5,6},{6,7},{7,4},{8,9},{9,10},{10,1... | collective-permute-start | bytes 1572872 | tf_op jit(solution)/shard_map/ppermute | solution.py:22
  94.0 8.2 %collective-permute-start.15 = (bf16[64,2048]{1,0:T(8,128)(2,1)S(1)}, bf16[64,2048]{1,0:T(8,128)(2,1)S(1)}, u32[]{:S(2)}, u32[]{:S(2)}) collective-permute-start(bf16[64,2048]{1,0:T(8,128)(2,1)S(1)} %get-tuple-element.20), channel_id=1, source_target_pairs={{0,3},{1,0},{2,1},{3,2},{4,7},{5,4},{6,5},{7,6},{8,11},{9,8},{10,9... | collective-permute-start | bytes 786440 | tf_op jit(solution)/shard_map/ppermute | solution.py:22
  95.9 6.4 %collective-permute-start.16 = (bf16[64,2048]{1,0:T(8,128)(2,1)S(1)}, bf16[64,2048]{1,0:T(8,128)(2,1)S(1)}, u32[]{:S(2)}, u32[]{:S(2)}) collective-permute-start(bf16[64,2048]{1,0:T(8,128)(2,1)S(1)} %slice.85), channel_id=1, source_target_pairs={{0,1},{1,2},{2,3},{3,0},{4,5},{5,6},{6,7},{7,4},{8,9},{9,10},{10,1... | collective-permute-start | bytes 786440 | tf_op jit(solution)/shard_map/ppermute | solution.py:22
  96.9 11.8 %collective-permute-start.14 = (f32[192,512]{1,0:T(8,128)S(1)}, f32[192,512]{1,0:T(8,128)S(1)}, u32[]{:S(2)}, u32[]{:S(2)}) collective-permute-start(f32[192,512]{1,0:T(8,128)S(1)} %pad_maximum_fusion.8), channel_id=1, source_target_pairs={{0,16},{16,0},{1,17},{17,1},{2,18},{18,2},{3,19},{19,3},{4,20},{20... | collective-permute-start | bytes 1179656 | tf_op jit(solution)/shard_map/ppermute | solution.py:18
  102.9 6.7 %collective-permute-start.17 = (f32[64,512]{1,0:T(8,128)S(1)}, f32[64,512]{1,0:T(8,128)S(1)}, u32[]{:S(2)}, u32[]{:S(2)}) collective-permute-start(f32[64,512]{1,0:T(8,128)S(1)} %fusion.20), channel_id=1, source_target_pairs={{0,16},{16,0},{1,17},{17,1},{2,18},{18,2},{3,19},{19,3},{4,20},{20... | collective-permute-start | bytes 393224 | tf_op jit(solution)/shard_map/ppermute | solution.py:18
  110.2 7.6 %collective-permute-start.18 = (bf16[256,512]{1,0:T(8,128)(2,1)S(1)}, bf16[256,512]{1,0:T(8,128)(2,1)S(1)}, u32[]{:S(2)}, u32[]{:S(2)}) collective-permute-start(bf16[256,512]{1,0:T(8,128)(2,1)S(1)} %dynamic-slice_convert_fusion), channel_id=1, source_target_pairs={{0,32},{32,0},{1,33},{33,1},{2,34},{34,2},{3,35},{35,3},{4,36},{36... | collective-permute-start | bytes 786440 | tf_op jit(solution)/shard_map/ppermute | solution.py:18
  110.6 11.9 %collective-permute-start.19 = (bf16[256,512]{1,0:T(8,128)(2,1)S(1)}, bf16[256,512]{1,0:T(8,128)(2,1)S(1)}, u32[]{:S(2)}, u32[]{:S(2)}) collective-permute-start(bf16[256,512]{1,0:T(8,128)(2,1)S(1)} %dynamic-slice_convert_fusion), channel_id=1, source_target_pairs={{0,128},{64,192},{128,0},{192,64},{1,129},{65,193},{129,1},{193,65... | collective-permute-start | bytes 786440 | tf_op jit(solution)/shard_map/ppermute | solution.py:22
  117.9 13.4 %collective-permute-start.20 = (bf16[512,512]{1,0:T(8,128)(2,1)S(1)}, bf16[512,512]{1,0:T(8,128)(2,1)S(1)}, u32[]{:S(2)}, u32[]{:S(2)}) collective-permute-start(bf16[512,512]{1,0:T(8,128)(2,1)S(1)} %pad_maximum_fusion.7), channel_id=1, source_target_pairs={{0,64},{64,0},{128,192},{192,128},{1,65},{65,1},{129,193},{193,129... | collective-permute-start | bytes 1572872 | tf_op jit(solution)/shard_map/ppermute | solution.py:35
  119.0 14.3 %collective-permute-start.21 = (bf16[512,512]{1,0:T(8,128)(2,1)S(1)}, bf16[512,512]{1,0:T(8,128)(2,1)S(1)}, u32[]{:S(2)}, u32[]{:S(2)}) collective-permute-start(bf16[512,512]{1,0:T(8,128)(2,1)S(1)} %pad_maximum_fusion.7), channel_id=1, source_target_pairs={{0,192},{64,128},{128,64},{192,0},{1,193},{65,129},{129,65},{193,1... | collective-permute-start | bytes 1572872 | tf_op jit(solution)/shard_map/ppermute | solution.py:35
  122.6 6.0 %collective-permute-start.22 = (bf16[256,512]{1,0:T(8,128)(2,1)S(1)}, bf16[256,512]{1,0:T(8,128)(2,1)S(1)}, u32[]{:S(2)}, u32[]{:S(2)}) collective-permute-start(bf16[256,512]{1,0:T(8,128)(2,1)S(1)} %collective-permute-done.19), channel_id=1, source_target_pairs={{0,32},{32,0},{1,33},{33,1},{2,34},{34,2},{3,35},{35,3},{4,36},{36... | collective-permute-start | bytes 786440 | tf_op jit(solution)/shard_map/ppermute | solution.py:18
  134.4 3.7 %collective-permute-start.23 = (f32[256,512]{1,0:T(8,128)S(1)}, f32[256,512]{1,0:T(8,128)S(1)}, u32[]{:S(2)}, u32[]{:S(2)}) collective-permute-start(f32[256,512]{1,0:T(8,128)S(1)} %convolution_add_fusion), channel_id=1, source_target_pairs={{0,16},{16,0},{1,17},{17,1},{2,18},{18,2},{3,19},{19,3},{4,20},{20... | collective-permute-start | bytes 1572872 | tf_op jit(solution)/shard_map/ppermute | solution.py:18
where the time goes:
time: 140 us; the launch traced here: 139 us
  waiting for transfers between devices  53.2 us (38%)
  starting transfers between devices  53.1 us (38%)
  blocking collectives  15.8 us (11%)
  matrix products  10.1 us (7%)
  other arithmetic  5.01 us (4%)
  local copies, waits for them, and re-layouts  1.71 us (1%)
    ppermute x10, waiting for transfers between devices, trade(): return lax.ppermute(array, axis, [(i, i ^ k) for i in range(4)])  29.8 us
    ppermute x8, starting transfers between devices, swap(): return lax.ppermute(array, axis, [(0, 1), (1, 0)])  18.6 us
    ppermute x10, starting transfers between devices, trade(): return lax.ppermute(array, axis, [(i, i ^ k) for i in range(4)])  16.8 us
    all_gather x1, blocking collectives, per_device(): near = lax.all_gather(part, 'zh', axis=0, tiled=True)  15.8 us
    ppermute x8, waiting for transfers between devices, swap(): return lax.ppermute(array, axis, [(0, 1), (1, 0)])  14.8 us
    ppermute x6, starting transfers between devices, send(): lax.ppermute(array, axis, [(i, (i + k) % 4) for i in range(4)])  13.6 us
    dot_general x14, matrix products, matmul(): return lax.dot_general(a, b, (dims, ((), ())), preferred_element_type=F32)  10.1 us
    ppermute x6, waiting for transfers between devices, send(): lax.ppermute(array, axis, [(i, (i + k) % 4) for i in range(4)])  8.59 us
  transfers between devices with their start and end apart: 25, of which 18 were waited for; matrix products, arithmetic and copies ran while one was open for 8% of the time, Pallas kernels for 0%

commit v1 on v0

--- a/solution.py
+++ b/solution.py
@@ -12,6 +12,11 @@
 ROW = ("x", "zl", "core")
 COL = ("zh", "y")
 BF, F32 = (jnp.bfloat16, jnp.float32)
+
+
+def gather_over(x, axis, dim):
+    repeated = jnp.stack([x] * lax.axis_size(axis))
+    return jnp.concatenate(lax.all_to_all(repeated, axis, 0, 0), axis=dim)
 
 
 def swap(array, axis):
@@ -91,7 +96,7 @@
     part = jnp.concatenate([first, second], axis=1)
     panel = jnp.concatenate([early, panel], axis=0)
     part = add(scatter_pairs(chunks(part), "zh"))
-    near = lax.all_gather(part, "zh", axis=0, tiled=True)
+    near = gather_over(part, "zh", 0)
     after, before = (fetch(near, "y", 1), fetch(near, "y", 3))
     sent = lax.optimization_barrier((after[:64], before[64:]))
     far = lax.optimization_barrier((fetch(sent[0], "y", 1), fetch(sent[1], "y", 3)))

time: 140 us -> 144 us (1.029)
  waiting for transfers between devices: 53.2 us -> 77.3 us
  blocking collectives: 15.8 us -> 0 us
  starting transfers between devices: 53.1 us -> 49.2 us
    all_gather x1 -> x0, blocking collectives: 15.8 us -> none  [per_device(): near = lax.all_gather(part, 'zh', axis=0, tiled=True)]
    all_to_all x0 -> x1, waiting for transfers between devices: none -> 11.5 us  [gather_over(): return jnp.concatenate(lax.all_to_all(repeated, axis, 0, 0), axis=dim)]
    ppermute x6, waiting for transfers between devices: 8.59 us -> 16.5 us  [send(): lax.ppermute(array, axis, [(i, (i + k) % 4) for i in range(4)])]
    all_to_all x0 -> x1, starting transfers between devices: none -> 6.36 us  [gather_over(): return jnp.concatenate(lax.all_to_all(repeated, axis, 0, 0), axis=dim)]
    ppermute x8, starting transfers between devices: 18.6 us -> 13 us  [swap(): return lax.ppermute(array, axis, [(0, 1), (1, 0)])]
    ppermute x10, starting transfers between devices: 16.8 us -> 12.2 us  [trade(): return lax.ppermute(array, axis, [(i, i ^ k) for i in range(4)])]
    ppermute x8, waiting for transfers between devices: 14.8 us -> 18 us  [swap(): return lax.ppermute(array, axis, [(0, 1), (1, 0)])]
    ppermute x10, waiting for transfers between devices: 29.8 us -> 31.3 us  [trade(): return lax.ppermute(array, axis, [(i, i ^ k) for i in range(4)])]
  transfers between devices with their start and end apart: 25 -> 26, of which waited for: 18 -> 21; matrix products, arithmetic and copies ran while one was open for 8% -> 8% of each run, Pallas kernels for 0% -> 0%
where the time goes in v1:
time: 144 us
  waiting for transfers between devices  77.3 us (54%)
  starting transfers between devices  49.2 us (34%)
  matrix products  10.1 us (7%)
  other arithmetic  4.11 us (3%)
  local copies, waits for them, and re-layouts  2.59 us (2%)
    ppermute x10, waiting for transfers between devices, trade(): return lax.ppermute(array, axis, [(i, i ^ k) for i in range(4)])  31.3 us
    ppermute x8, waiting for transfers between devices, swap(): return lax.ppermute(array, axis, [(0, 1), (1, 0)])  18 us
    ppermute x6, waiting for transfers between devices, send(): lax.ppermute(array, axis, [(i, (i + k) % 4) for i in range(4)])  16.5 us
    ppermute x6, starting transfers between devices, send(): lax.ppermute(array, axis, [(i, (i + k) % 4) for i in range(4)])  13.5 us
    ppermute x8, starting transfers between devices, swap(): return lax.ppermute(array, axis, [(0, 1), (1, 0)])  13 us
    ppermute x10, starting transfers between devices, trade(): return lax.ppermute(array, axis, [(i, i ^ k) for i in range(4)])  12.2 us
    all_to_all x1, waiting for transfers between devices, gather_over(): return jnp.concatenate(lax.all_to_all(repeated, axis, 0, 0), axis=dim)  11.5 us
    dot_general x14, matrix products, matmul(): return lax.dot_general(a, b, (dims, ((), ())), preferred_element_type=F32)  10.1 us
  transfers between devices with their start and end apart: 26, of which 21 were waited for; matrix products, arithmetic and copies ran while one was open for 8% of the time, Pallas kernels for 0%

profile of v1, /device:TPU:1, one launch (start us, length us, event | category | flops | bytes accessed | tf_op | source)
XLA Modules:
  0.0 143.8 jit_solution(15963387889569627992)
XLA Ops:
  0.0 3.2 %collective-permute-start.1 = (bf16[256,512]{1,0:T(8,128)(2,1)}, bf16[256,512]{1,0:T(8,128)(2,1)S(1)}, u32[]{:S(2)}, u32[]{:S(2)}) collective-permute-start(bf16[256,512]{1,0:T(8,128)(2,1)} %param.1), channel_id=1, source_target_pairs={{0,16},{16,0},{1,17},{17,1},{2,18},{18,2},{3,19},{19,3},{4,20},{20... | collective-permute-start | bytes 786440 | tf_op jit(solution)/shard_map/ppermute | solution.py:23
  3.2 2.6 %collective-permute-start.2 = (bf16[256,512]{1,0:T(8,128)(2,1)}, bf16[256,512]{1,0:T(8,128)(2,1)}, u32[]{:S(2)}, u32[]{:S(2)}) collective-permute-start(bf16[256,512]{1,0:T(8,128)(2,1)} %param.1), channel_id=1, source_target_pairs={{0,128},{64,192},{128,0},{192,64},{1,129},{65,193},{129,1},{193,65... | collective-permute-start | bytes 786440 | tf_op jit(solution)/shard_map/ppermute | solution.py:27
  7.3 4.2 %collective-permute-done = bf16[256,512]{1,0:T(8,128)(2,1)S(1)} collective-permute-done((bf16[256,512]{1,0:T(8,128)(2,1)}, bf16[256,512]{1,0:T(8,128)(2,1)S(1)}, u32[]{:S(2)}, u32[]{:S(2)}) %collective-permute-start) | collective-permute-done | bytes 262176 | tf_op jit(solution)/shard_map/ppermute | solution.py:23
  11.6 1.6 %collective-permute-start.4 = (bf16[512,512]{1,0:T(8,128)(2,1)S(1)}, bf16[512,512]{1,0:T(8,128)(2,1)}, u32[]{:S(2)}, u32[]{:S(2)}) collective-permute-start(bf16[512,512]{1,0:T(8,128)(2,1)S(1)} %pad_maximum_fusion.3), channel_id=1, source_target_pairs={{0,192},{64,128},{128,64},{192,0},{1,193},{65,129},{129,65},{193,1... | collective-permute-start | bytes 1572872 | tf_op jit(solution)/shard_map/ppermute | solution.py:40
  14.2 1.5 %collective-permute-start.5 = (bf16[256,512]{1,0:T(8,128)(2,1)}, bf16[256,512]{1,0:T(8,128)(2,1)}, u32[]{:S(2)}, u32[]{:S(2)}) collective-permute-start(bf16[256,512]{1,0:T(8,128)(2,1)} %collective-permute-done.2), channel_id=1, source_target_pairs={{0,32},{32,0},{1,33},{33,1},{2,34},{34,2},{3,35},{35,3},{4,36},{36... | collective-permute-start | bytes 786440 | tf_op jit(solution)/shard_map/ppermute | solution.py:23
  15.7 1.5 %convolution_convert_fusion.4 = bf16[512,768]{1,0:T(8,128)(2,1)} fusion(bf16[512,512]{1,0:T(8,128)(2,1)S(1)} %bitcast.34, bf16[768,512]{1,0:T(8,128)(2,1)S(1)} %pad_maximum_fusion.2), kind=kOutput, calls=%fused_computation.5 | convolution fusion | flops 403046400 | bytes 2097152 | tf_op jit(solution)/shard_map/dot_general | solution.py:58
  17.2 4.2 %all-to-all-start = ((bf16[4,128,768]{2,1,0:T(8,128)(2,1)}), bf16[4,128,768]{2,1,0:T(8,128)(2,1)S(1)}, u32[]{:S(2)}, u32[]{:S(2)}) async-start(bf16[4,128,768]{2,1,0:T(8,128)(2,1)} %bitcast.35), calls=%async_computation | async-start | bytes 1572864 | tf_op jit(solution)/shard_map/all_to_all | solution.py:91
  21.3 3.2 %collective-permute-done.3 = bf16[512,512]{1,0:T(8,128)(2,1)S(1)} collective-permute-done((bf16[512,512]{1,0:T(8,128)(2,1)S(1)}, bf16[512,512]{1,0:T(8,128)(2,1)S(1)}, u32[]{:S(2)}, u32[]{:S(2)}) %collective-permute-start.3) | collective-permute-done | bytes 524320 | tf_op jit(solution)/shard_map/ppermute | solution.py:40
  24.5 1.3 collective-permute-done.4
  29.7 1.9 %collective-permute-start.7 = (bf16[128,1280]{1,0:T(8,128)(2,1)S(1)}, bf16[128,1280]{1,0:T(8,128)(2,1)}, u32[]{:S(2)}, u32[]{:S(2)}) collective-permute-start(bf16[128,1280]{1,0:T(8,128)(2,1)S(1)} %convolution_convert_fusion.1), channel_id=1, source_target_pairs={{0,3},{1,2},{2,1},{3,0},{4,7},{5,6},{6,5},{7,4},{8,11},{9,10},{10,... | collective-permute-start | bytes 983048 | tf_op jit(solution)/shard_map/ppermute | solution.py:40
  34.3 4.3 %collective-permute-done.6 = bf16[128,1280]{1,0:T(8,128)(2,1)} collective-permute-done((bf16[128,1280]{1,0:T(8,128)(2,1)}, bf16[128,1280]{1,0:T(8,128)(2,1)}, u32[]{:S(2)}, u32[]{:S(2)}) %collective-permute-start.6) | collective-permute-done | bytes 327712 | tf_op jit(solution)/shard_map/ppermute | solution.py:40
  39.3 7.1 %collective-permute-done.8 = bf16[128,1280]{1,0:T(8,128)(2,1)} collective-permute-done((bf16[128,1280]{1,0:T(8,128)(2,1)}, bf16[128,1280]{1,0:T(8,128)(2,1)}, u32[]{:S(2)}, u32[]{:S(2)}) %collective-permute-start.8) | collective-permute-done | bytes 327712 | tf_op jit(solution)/shard_map/ppermute | solution.py:40
  46.5 1.3 add_convert_fusion
  47.8 4.8 %collective-permute-start.10 = (bf16[32,2048]{1,0:T(8,128)(2,1)S(1)}, bf16[32,2048]{1,0:T(8,128)(2,1)S(1)}, u32[]{:S(2)}, u32[]{:S(2)}) collective-permute-start(bf16[32,2048]{1,0:T(8,128)(2,1)S(1)} %get-tuple-element.37), channel_id=1, source_target_pairs={{0,12},{4,8},{8,4},{12,0},{1,13},{5,9},{9,5},{13,1},{2,14},{6,10},... | collective-permute-start | bytes 393224 | tf_op jit(solution)/shard_map/ppermute | solution.py:40
  52.6 1.6 %collective-permute-start.11 = (bf16[32,2048]{1,0:T(8,128)(2,1)S(1)}, bf16[32,2048]{1,0:T(8,128)(2,1)S(1)}, u32[]{:S(2)}, u32[]{:S(2)}) collective-permute-start(bf16[32,2048]{1,0:T(8,128)(2,1)S(1)} %get-tuple-element.36), channel_id=1, source_target_pairs={{0,8},{4,12},{8,0},{12,4},{1,9},{5,13},{9,1},{13,5},{2,10},{6,14},... | collective-permute-start | bytes 393224 | tf_op jit(solution)/shard_map/ppermute | solution.py:40
  54.8 7.3 %collective-permute-done.10 = bf16[32,2048]{1,0:T(8,128)(2,1)S(1)} collective-permute-done((bf16[32,2048]{1,0:T(8,128)(2,1)S(1)}, bf16[32,2048]{1,0:T(8,128)(2,1)S(1)}, u32[]{:S(2)}, u32[]{:S(2)}) %collective-permute-start.10) | collective-permute-done | bytes 131104 | tf_op jit(solution)/shard_map/ppermute | solution.py:40
  64.1 6.4 %all-to-all-start.1 = ((bf16[4,32,2048]{2,1,0:T(8,128)(2,1)}), bf16[4,32,2048]{2,1,0:T(8,128)(2,1)S(1)}, u32[]{:S(2)}, u32[]{:S(2)}) async-start(bf16[4,32,2048]{2,1,0:T(8,128)(2,1)} %stack.27), calls=%async_computation.1 | async-start | bytes 1048576 | tf_op jit(solution)/shard_map/all_to_all | solution.py:19
  70.5 11.5 %all-to-all-done.1 = bf16[4,32,2048]{2,1,0:T(8,128)(2,1)S(1)} async-done(((bf16[4,32,2048]{2,1,0:T(8,128)(2,1)}), bf16[4,32,2048]{2,1,0:T(8,128)(2,1)S(1)}, u32[]{:S(2)}, u32[]{:S(2)}) %all-to-all-start.1) | async-done | bytes 524320 | tf_op jit(solution)/shard_map/all_to_all | solution.py:19
  81.9 1.7 %collective-permute-start.12 = (bf16[128,2048]{1,0:T(8,128)(2,1)S(1)}, bf16[128,2048]{1,0:T(8,128)(2,1)S(1)}, u32[]{:S(2)}, u32[]{:S(2)}) collective-permute-start(bf16[128,2048]{1,0:T(8,128)(2,1)S(1)} %bitcast.30), channel_id=1, source_target_pairs={{0,3},{1,0},{2,1},{3,2},{4,7},{5,4},{6,5},{7,6},{8,11},{9,8},{10,9... | collective-permute-start | bytes 1572872 | tf_op jit(solution)/shard_map/ppermute | solution.py:27
  83.7 7.1 %collective-permute-start.13 = (bf16[128,2048]{1,0:T(8,128)(2,1)S(1)}, bf16[128,2048]{1,0:T(8,128)(2,1)S(1)}, u32[]{:S(2)}, u32[]{:S(2)}) collective-permute-start(bf16[128,2048]{1,0:T(8,128)(2,1)S(1)} %bitcast.31), channel_id=1, source_target_pairs={{0,1},{1,2},{2,3},{3,0},{4,5},{5,6},{6,7},{7,4},{8,9},{9,10},{10,1... | collective-permute-start | bytes 1572872 | tf_op jit(solution)/shard_map/ppermute | solution.py:27
  91.4 9.9 %collective-permute-done.13 = bf16[128,2048]{1,0:T(8,128)(2,1)S(1)} collective-permute-done((bf16[128,2048]{1,0:T(8,128)(2,1)S(1)}, bf16[128,2048]{1,0:T(8,128)(2,1)S(1)}, u32[]{:S(2)}, u32[]{:S(2)}) %collective-permute-start.13) | collective-permute-done | bytes 524320 | tf_op jit(solution)/shard_map/ppermute | solution.py:27
  102.4 1.9 %collective-permute-start.15 = (bf16[64,2048]{1,0:T(8,128)(2,1)S(1)}, bf16[64,2048]{1,0:T(8,128)(2,1)S(1)}, u32[]{:S(2)}, u32[]{:S(2)}) collective-permute-start(bf16[64,2048]{1,0:T(8,128)(2,1)S(1)} %get-tuple-element.20), channel_id=1, source_target_pairs={{0,3},{1,0},{2,1},{3,2},{4,7},{5,4},{6,5},{7,6},{8,11},{9,8},{10,9... | collective-permute-start | bytes 786440 | tf_op jit(solution)/shard_map/ppermute | solution.py:27
  105.3 2.0 %collective-permute-start.14 = (f32[192,512]{1,0:T(8,128)S(1)}, f32[192,512]{1,0:T(8,128)S(1)}, u32[]{:S(2)}, u32[]{:S(2)}) collective-permute-start(f32[192,512]{1,0:T(8,128)S(1)} %pad_maximum_fusion.8), channel_id=1, source_target_pairs={{0,16},{16,0},{1,17},{17,1},{2,18},{18,2},{3,19},{19,3},{4,20},{20... | collective-permute-start | bytes 1179656 | tf_op jit(solution)/shard_map/ppermute | solution.py:23
  107.3 1.7 %collective-permute-done.15 = bf16[64,2048]{1,0:T(8,128)(2,1)S(1)} collective-permute-done((bf16[64,2048]{1,0:T(8,128)(2,1)S(1)}, bf16[64,2048]{1,0:T(8,128)(2,1)S(1)}, u32[]{:S(2)}, u32[]{:S(2)}) %collective-permute-start.15) | collective-permute-done | bytes 262176 | tf_op jit(solution)/shard_map/ppermute | solution.py:27
  109.0 2.4 %collective-permute-done.16 = bf16[64,2048]{1,0:T(8,128)(2,1)S(1)} collective-permute-done((bf16[64,2048]{1,0:T(8,128)(2,1)S(1)}, bf16[64,2048]{1,0:T(8,128)(2,1)S(1)}, u32[]{:S(2)}, u32[]{:S(2)}) %collective-permute-start.16) | collective-permute-done | bytes 262176 | tf_op jit(solution)/shard_map/ppermute | solution.py:27
  112.0 2.9 %collective-permute-start.17 = (f32[64,512]{1,0:T(8,128)S(1)}, f32[64,512]{1,0:T(8,128)S(1)}, u32[]{:S(2)}, u32[]{:S(2)}) collective-permute-start(f32[64,512]{1,0:T(8,128)S(1)} %fusion.20), channel_id=1, source_target_pairs={{0,16},{16,0},{1,17},{17,1},{2,18},{18,2},{3,19},{19,3},{4,20},{20... | collective-permute-start | bytes 393224 | tf_op jit(solution)/shard_map/ppermute | solution.py:23
  116.7 7.4 %collective-permute-done.18 = bf16[256,512]{1,0:T(8,128)(2,1)S(1)} collective-permute-done((bf16[256,512]{1,0:T(8,128)(2,1)S(1)}, bf16[256,512]{1,0:T(8,128)(2,1)S(1)}, u32[]{:S(2)}, u32[]{:S(2)}) %collective-permute-start.18) | collective-permute-done | bytes 262176 | tf_op jit(solution)/shard_map/ppermute | solution.py:23
  124.3 1.4 collective-permute-done.19
  126.9 4.6 %collective-permute-done.22 = bf16[256,512]{1,0:T(8,128)(2,1)S(1)} collective-permute-done((bf16[256,512]{1,0:T(8,128)(2,1)S(1)}, bf16[256,512]{1,0:T(8,128)(2,1)S(1)}, u32[]{:S(2)}, u32[]{:S(2)}) %collective-permute-start.22) | collective-permute-done | bytes 262176 | tf_op jit(solution)/shard_map/ppermute | solution.py:23
  131.5 4.9 %collective-permute-done.20 = bf16[512,512]{1,0:T(8,128)(2,1)S(1)} collective-permute-done((bf16[512,512]{1,0:T(8,128)(2,1)S(1)}, bf16[512,512]{1,0:T(8,128)(2,1)S(1)}, u32[]{:S(2)}, u32[]{:S(2)}) %collective-permute-start.20) | collective-permute-done | bytes 524320 | tf_op jit(solution)/shard_map/ppermute | solution.py:40
  136.4 1.3 collective-permute-done.21
  138.8 2.2 %collective-permute-start.23 = (f32[256,512]{1,0:T(8,128)S(1)}, f32[256,512]{1,0:T(8,128)S(1)}, u32[]{:S(2)}, u32[]{:S(2)}) collective-permute-start(f32[256,512]{1,0:T(8,128)S(1)} %convolution_add_fusion), channel_id=1, source_target_pairs={{0,16},{16,0},{1,17},{17,1},{2,18},{18,2},{3,19},{19,3},{4,20},{20... | collective-permute-start | bytes 1572872 | tf_op jit(solution)/shard_map/ppermute | solution.py:23
  (88 shorter events, 22.4 us)
Async XLA Ops:
  0.0 6.8 %collective-permute-start.1 = (bf16[256,512]{1,0:T(8,128)(2,1)}, bf16[256,512]{1,0:T(8,128)(2,1)S(1)}, u32[]{:S(2)}, u32[]{:S(2)}) collective-permute-start(bf16[256,512]{1,0:T(8,128)(2,1)} %param.1), channel_id=1, source_target_pairs={{0,16},{16,0},{1,17},{17,1},{2,18},{18,2},{3,19},{19,3},{4,20},{20... | collective-permute-start | bytes 786440 | tf_op jit(solution)/shard_map/ppermute | solution.py:23
  3.2 8.3 %collective-permute-start = (bf16[256,512]{1,0:T(8,128)(2,1)}, bf16[256,512]{1,0:T(8,128)(2,1)S(1)}, u32[]{:S(2)}, u32[]{:S(2)}) collective-permute-start(bf16[256,512]{1,0:T(8,128)(2,1)} %param.1), channel_id=1, source_target_pairs={{0,32},{32,0},{1,33},{33,1},{2,34},{34,2},{3,35},{35,3},{4,36},{36... | collective-permute-start | bytes 786440 | tf_op jit(solution)/shard_map/ppermute | solution.py:23
  3.2 9.9 %collective-permute-start.2 = (bf16[256,512]{1,0:T(8,128)(2,1)}, bf16[256,512]{1,0:T(8,128)(2,1)}, u32[]{:S(2)}, u32[]{:S(2)}) collective-permute-start(bf16[256,512]{1,0:T(8,128)(2,1)} %param.1), channel_id=1, source_target_pairs={{0,128},{64,192},{128,0},{192,64},{1,129},{65,193},{129,1},{193,65... | collective-permute-start | bytes 786440 | tf_op jit(solution)/shard_map/ppermute | solution.py:27
  7.1 4.4 %copy-start = (bf16[256,512]{1,0:T(8,128)(2,1)S(1)}, bf16[256,512]{1,0:T(8,128)(2,1)}, u32[]{:S(2)}) copy-start(bf16[256,512]{1,0:T(8,128)(2,1)} %param.1) | copy-start | bytes 786436
  11.5 13.0 %collective-permute-start.3 = (bf16[512,512]{1,0:T(8,128)(2,1)S(1)}, bf16[512,512]{1,0:T(8,128)(2,1)S(1)}, u32[]{:S(2)}, u32[]{:S(2)}) collective-permute-start(bf16[512,512]{1,0:T(8,128)(2,1)S(1)} %pad_maximum_fusion.3), channel_id=1, source_target_pairs={{0,64},{64,0},{128,192},{192,128},{1,65},{65,1},{129,193},{193,129... | collective-permute-start | bytes 1572872 | tf_op jit(solution)/shard_map/ppermute | solution.py:40
  11.6 14.2 %collective-permute-start.4 = (bf16[512,512]{1,0:T(8,128)(2,1)S(1)}, bf16[512,512]{1,0:T(8,128)(2,1)}, u32[]{:S(2)}, u32[]{:S(2)}) collective-permute-start(bf16[512,512]{1,0:T(8,128)(2,1)S(1)} %pad_maximum_fusion.3), channel_id=1, source_target_pairs={{0,192},{64,128},{128,64},{192,0},{1,193},{65,129},{129,65},{193,1... | collective-permute-start | bytes 1572872 | tf_op jit(solution)/shard_map/ppermute | solution.py:40
  14.2 3.0 %copy-start.1 = (bf16[768,512]{1,0:T(8,128)(2,1)}, bf16[768,512]{1,0:T(8,128)(2,1)S(1)}, u32[]{:S(2)}) copy-start(bf16[768,512]{1,0:T(8,128)(2,1)S(1)} %pad_maximum_fusion.2) | copy-start | bytes 2359300
  14.2 7.1 %collective-permute-start.5 = (bf16[256,512]{1,0:T(8,128)(2,1)}, bf16[256,512]{1,0:T(8,128)(2,1)}, u32[]{:S(2)}, u32[]{:S(2)}) collective-permute-start(bf16[256,512]{1,0:T(8,128)(2,1)} %collective-permute-done.2), channel_id=1, source_target_pairs={{0,32},{32,0},{1,33},{33,1},{2,34},{34,2},{3,35},{35,3},{4,36},{36... | collective-permute-start | bytes 786440 | tf_op jit(solution)/shard_map/ppermute | solution.py:23
  17.2 17.0 %all-to-all-start = ((bf16[4,128,768]{2,1,0:T(8,128)(2,1)}), bf16[4,128,768]{2,1,0:T(8,128)(2,1)S(1)}, u32[]{:S(2)}, u32[]{:S(2)}) async-start(bf16[4,128,768]{2,1,0:T(8,128)(2,1)} %bitcast.35), calls=%async_computation | async-start | bytes 1572864 | tf_op jit(solution)/shard_map/all_to_all | solution.py:91
  28.9 9.6 %collective-permute-start.6 = (bf16[128,1280]{1,0:T(8,128)(2,1)}, bf16[128,1280]{1,0:T(8,128)(2,1)}, u32[]{:S(2)}, u32[]{:S(2)}) collective-permute-start(bf16[128,1280]{1,0:T(8,128)(2,1)} %convolution_convert_fusion.2), channel_id=1, source_target_pairs={{0,1},{1,0},{2,3},{3,2},{4,5},{5,4},{6,7},{7,6},{8,9},{9,8},{10,11... | collective-permute-start | bytes 983048 | tf_op jit(solution)/shard_map/ppermute | solution.py:40
  29.7 9.6 %collective-permute-start.7 = (bf16[128,1280]{1,0:T(8,128)(2,1)S(1)}, bf16[128,1280]{1,0:T(8,128)(2,1)}, u32[]{:S(2)}, u32[]{:S(2)}) collective-permute-start(bf16[128,1280]{1,0:T(8,128)(2,1)S(1)} %convolution_convert_fusion.1), channel_id=1, source_target_pairs={{0,3},{1,2},{2,1},{3,0},{4,7},{5,6},{6,5},{7,4},{8,11},{9,10},{10,... | collective-permute-start | bytes 983048 | tf_op jit(solution)/shard_map/ppermute | solution.py:40
  32.9 13.6 %collective-permute-start.8 = (bf16[128,1280]{1,0:T(8,128)(2,1)}, bf16[128,1280]{1,0:T(8,128)(2,1)}, u32[]{:S(2)}, u32[]{:S(2)}) collective-permute-start(bf16[128,1280]{1,0:T(8,128)(2,1)} %convolution_convert_fusion), channel_id=1, source_target_pairs={{0,2},{1,3},{2,0},{3,1},{4,6},{5,7},{6,4},{7,5},{8,10},{9,11},{10,... | collective-permute-start | bytes 983048 | tf_op jit(solution)/shard_map/ppermute | solution.py:40
  47.8 14.3 %collective-permute-start.10 = (bf16[32,2048]{1,0:T(8,128)(2,1)S(1)}, bf16[32,2048]{1,0:T(8,128)(2,1)S(1)}, u32[]{:S(2)}, u32[]{:S(2)}) collective-permute-start(bf16[32,2048]{1,0:T(8,128)(2,1)S(1)} %get-tuple-element.37), channel_id=1, source_target_pairs={{0,12},{4,8},{8,4},{12,0},{1,13},{5,9},{9,5},{13,1},{2,14},{6,10},... | collective-permute-start | bytes 393224 | tf_op jit(solution)/shard_map/ppermute | solution.py:40
  52.6 9.8 %collective-permute-start.11 = (bf16[32,2048]{1,0:T(8,128)(2,1)S(1)}, bf16[32,2048]{1,0:T(8,128)(2,1)S(1)}, u32[]{:S(2)}, u32[]{:S(2)}) collective-permute-start(bf16[32,2048]{1,0:T(8,128)(2,1)S(1)} %get-tuple-element.36), channel_id=1, source_target_pairs={{0,8},{4,12},{8,0},{12,4},{1,9},{5,13},{9,1},{13,5},{2,10},{6,14},... | collective-permute-start | bytes 393224 | tf_op jit(solution)/shard_map/ppermute | solution.py:40
  54.2 9.0 %collective-permute-start.9 = (bf16[32,2048]{1,0:T(8,128)(2,1)S(1)}, bf16[32,2048]{1,0:T(8,128)(2,1)S(1)}, u32[]{:S(2)}, u32[]{:S(2)}) collective-permute-start(bf16[32,2048]{1,0:T(8,128)(2,1)S(1)} %get-tuple-element.35), channel_id=1, source_target_pairs={{0,4},{4,0},{8,12},{12,8},{1,5},{5,1},{9,13},{13,9},{2,6},{6,2},{1... | collective-permute-start | bytes 393224 | tf_op jit(solution)/shard_map/ppermute | solution.py:40
  63.2 27.7 %copy-start.2 = (bf16[768,512]{1,0:T(8,128)(2,1)S(1)}, bf16[768,512]{1,0:T(8,128)(2,1)}, u32[]{:S(2)}) copy-start(bf16[768,512]{1,0:T(8,128)(2,1)} %copy-done.1) | copy-start | bytes 2359300
  64.1 17.8 %all-to-all-start.1 = ((bf16[4,32,2048]{2,1,0:T(8,128)(2,1)}), bf16[4,32,2048]{2,1,0:T(8,128)(2,1)S(1)}, u32[]{:S(2)}, u32[]{:S(2)}) async-start(bf16[4,32,2048]{2,1,0:T(8,128)(2,1)} %stack.27), calls=%async_computation.1 | async-start | bytes 1048576 | tf_op jit(solution)/shard_map/all_to_all | solution.py:19
  81.9 20.4 %collective-permute-start.12 = (bf16[128,2048]{1,0:T(8,128)(2,1)S(1)}, bf16[128,2048]{1,0:T(8,128)(2,1)S(1)}, u32[]{:S(2)}, u32[]{:S(2)}) collective-permute-start(bf16[128,2048]{1,0:T(8,128)(2,1)S(1)} %bitcast.30), channel_id=1, source_target_pairs={{0,3},{1,0},{2,1},{3,2},{4,7},{5,4},{6,5},{7,6},{8,11},{9,8},{10,9... | collective-permute-start | bytes 1572872 | tf_op jit(solution)/shard_map/ppermute | solution.py:27
  83.7 17.7 %collective-permute-start.13 = (bf16[128,2048]{1,0:T(8,128)(2,1)S(1)}, bf16[128,2048]{1,0:T(8,128)(2,1)S(1)}, u32[]{:S(2)}, u32[]{:S(2)}) collective-permute-start(bf16[128,2048]{1,0:T(8,128)(2,1)S(1)} %bitcast.31), channel_id=1, source_target_pairs={{0,1},{1,2},{2,3},{3,0},{4,5},{5,6},{6,7},{7,4},{8,9},{9,10},{10,1... | collective-permute-start | bytes 1572872 | tf_op jit(solution)/shard_map/ppermute | solution.py:27
  102.4 6.6 %collective-permute-start.15 = (bf16[64,2048]{1,0:T(8,128)(2,1)S(1)}, bf16[64,2048]{1,0:T(8,128)(2,1)S(1)}, u32[]{:S(2)}, u32[]{:S(2)}) collective-permute-start(bf16[64,2048]{1,0:T(8,128)(2,1)S(1)} %get-tuple-element.20), channel_id=1, source_target_pairs={{0,3},{1,0},{2,1},{3,2},{4,7},{5,4},{6,5},{7,6},{8,11},{9,8},{10,9... | collective-permute-start | bytes 786440 | tf_op jit(solution)/shard_map/ppermute | solution.py:27
  104.3 7.1 %collective-permute-start.16 = (bf16[64,2048]{1,0:T(8,128)(2,1)S(1)}, bf16[64,2048]{1,0:T(8,128)(2,1)S(1)}, u32[]{:S(2)}, u32[]{:S(2)}) collective-permute-start(bf16[64,2048]{1,0:T(8,128)(2,1)S(1)} %slice.93), channel_id=1, source_target_pairs={{0,1},{1,2},{2,3},{3,0},{4,5},{5,6},{6,7},{7,4},{8,9},{9,10},{10,1... | collective-permute-start | bytes 786440 | tf_op jit(solution)/shard_map/ppermute | solution.py:27
  105.3 9.7 %collective-permute-start.14 = (f32[192,512]{1,0:T(8,128)S(1)}, f32[192,512]{1,0:T(8,128)S(1)}, u32[]{:S(2)}, u32[]{:S(2)}) collective-permute-start(f32[192,512]{1,0:T(8,128)S(1)} %pad_maximum_fusion.8), channel_id=1, source_target_pairs={{0,16},{16,0},{1,17},{17,1},{2,18},{18,2},{3,19},{19,3},{4,20},{20... | collective-permute-start | bytes 1179656 | tf_op jit(solution)/shard_map/ppermute | solution.py:23
  112.0 3.9 %collective-permute-start.17 = (f32[64,512]{1,0:T(8,128)S(1)}, f32[64,512]{1,0:T(8,128)S(1)}, u32[]{:S(2)}, u32[]{:S(2)}) collective-permute-start(f32[64,512]{1,0:T(8,128)S(1)} %fusion.20), channel_id=1, source_target_pairs={{0,16},{16,0},{1,17},{17,1},{2,18},{18,2},{3,19},{19,3},{4,20},{20... | collective-permute-start | bytes 393224 | tf_op jit(solution)/shard_map/ppermute | solution.py:23
  116.5 7.6 %collective-permute-start.18 = (bf16[256,512]{1,0:T(8,128)(2,1)S(1)}, bf16[256,512]{1,0:T(8,128)(2,1)S(1)}, u32[]{:S(2)}, u32[]{:S(2)}) collective-permute-start(bf16[256,512]{1,0:T(8,128)(2,1)S(1)} %dynamic-slice_convert_fusion), channel_id=1, source_target_pairs={{0,32},{32,0},{1,33},{33,1},{2,34},{34,2},{3,35},{35,3},{4,36},{36... | collective-permute-start | bytes 786440 | tf_op jit(solution)/shard_map/ppermute | solution.py:23
  116.6 9.1 %collective-permute-start.19 = (bf16[256,512]{1,0:T(8,128)(2,1)S(1)}, bf16[256,512]{1,0:T(8,128)(2,1)S(1)}, u32[]{:S(2)}, u32[]{:S(2)}) collective-permute-start(bf16[256,512]{1,0:T(8,128)(2,1)S(1)} %dynamic-slice_convert_fusion), channel_id=1, source_target_pairs={{0,128},{64,192},{128,0},{192,64},{1,129},{65,193},{129,1},{193,65... | collective-permute-start | bytes 786440 | tf_op jit(solution)/shard_map/ppermute | solution.py:27
  124.1 12.3 %collective-permute-start.20 = (bf16[512,512]{1,0:T(8,128)(2,1)S(1)}, bf16[512,512]{1,0:T(8,128)(2,1)S(1)}, u32[]{:S(2)}, u32[]{:S(2)}) collective-permute-start(bf16[512,512]{1,0:T(8,128)(2,1)S(1)} %pad_maximum_fusion.7), channel_id=1, source_target_pairs={{0,64},{64,0},{128,192},{192,128},{1,65},{65,1},{129,193},{193,129... | collective-permute-start | bytes 1572872 | tf_op jit(solution)/shard_map/ppermute | solution.py:40
  124.2 13.5 %collective-permute-start.21 = (bf16[512,512]{1,0:T(8,128)(2,1)S(1)}, bf16[512,512]{1,0:T(8,128)(2,1)S(1)}, u32[]{:S(2)}, u32[]{:S(2)}) collective-permute-start(bf16[512,512]{1,0:T(8,128)(2,1)S(1)} %pad_maximum_fusion.7), channel_id=1, source_target_pairs={{0,192},{64,128},{128,64},{192,0},{1,193},{65,129},{129,65},{193,1... | collective-permute-start | bytes 1572872 | tf_op jit(solution)/shard_map/ppermute | solution.py:40
  125.7 5.8 %collective-permute-start.22 = (bf16[256,512]{1,0:T(8,128)(2,1)S(1)}, bf16[256,512]{1,0:T(8,128)(2,1)S(1)}, u32[]{:S(2)}, u32[]{:S(2)}) collective-permute-start(bf16[256,512]{1,0:T(8,128)(2,1)S(1)} %collective-permute-done.19), channel_id=1, source_target_pairs={{0,32},{32,0},{1,33},{33,1},{2,34},{34,2},{3,35},{35,3},{4,36},{36... | collective-permute-start | bytes 786440 | tf_op jit(solution)/shard_map/ppermute | solution.py:23
  138.8 3.7 %collective-permute-start.23 = (f32[256,512]{1,0:T(8,128)S(1)}, f32[256,512]{1,0:T(8,128)S(1)}, u32[]{:S(2)}, u32[]{:S(2)}) collective-permute-start(f32[256,512]{1,0:T(8,128)S(1)} %convolution_add_fusion), channel_id=1, source_target_pairs={{0,16},{16,0},{1,17},{17,1},{2,18},{18,2},{3,19},{19,3},{4,20},{20... | collective-permute-start | bytes 1572872 | tf_op jit(solution)/shard_map/ppermute | solution.py:23
